TPU v7x, 512 devices: a whole 4x4x16 slice. The times are simulated.
512 devices in a mesh: grp: 16 (over z_lo, core), seq: 32 (over x, z_hi, y).
Axes of the slice: x: 4, y: 4, z: 16 (z_hi: 2, z_lo: 8; z = z_hi * 8 + z_lo), core: 2. Of those that a mesh axis runs over, the one named last changes fastest.
Arguments:
- queries: bfloat16 [65536, 3072], P(('grp', 'seq')), may hold values from -6 to 6, as said below
- key_states: bfloat16 [65536, 3072], P(('grp', 'seq')), may hold values from -6 to 6
- value_states: bfloat16 [65536, 3072], P(('grp', 'seq')), may hold values from -16 to 16
- key_keep: int32 [65536], P(('grp', 'seq')), may hold values 0 or 1
- summary_pos: int32 [16], replicated, may hold values from 0 to 31
Outputs:
- attended: bfloat16 [65536, 3072], P(('grp', 'seq'))
Inputs may be any that keep to these rules, and one draw needn't show every extreme that they name: queries and key_states entries lie within -6 to 6.
All inputs are finite; a program needn't handle non-finite values. No bound on the sum of `key_keep` on one device may be relied on, other than what follows from the above.
Results may differ from a plain program's by a relative error of at most 0.008.
Values may be sent and summed in bfloat16 or wider, within the bound.
No kernel may reach another device: no remote copies, remote signals or barrier semaphores. Data moves between devices by JAX's collectives and lax.ppermute only.
A program may use at most 64 MiB of HBM per device.

v0:
```python
import math
import jax
import jax.numpy as jnp
from jax import lax
from jax.sharding import PartitionSpec as P

HEADS = 24
HEAD_DIM = 128
FIXED_HEADS = 4
STRIDED_HEADS = 4
LOCAL_HEADS = 16
BLOCK = 128
LOOKBACK = 2
NEG = -1e30


def passed_along(block, axis, distance):
    devices = range(lax.axis_size(axis))
    route = [(i - distance, i) for i in devices if i - distance in devices]
    return lax.ppermute(block, axis, route)


def spread(value, axis, source):
    kept = jnp.where(lax.axis_index(axis) == source, value, 0).astype(value.dtype)
    return lax.psum(kept, axis)


def partial_softmax(query_heads, key_rows, value_rows, allowed):
    scores = jnp.einsum(
        "qhd,khd->hqk", query_heads, key_rows, preferred_element_type=jnp.float32
    ) / math.sqrt(HEAD_DIM)
    scores = jnp.where(allowed[None], scores, NEG)
    row_max = jnp.max(scores, axis=2)
    weights = jnp.where(allowed[None], jnp.exp(scores - row_max[:, :, None]), 0.0)
    row_sum = jnp.sum(weights, axis=2)
    weighted = jnp.einsum(
        "hqk,khd->hqd", weights.astype(jnp.bfloat16), value_rows, preferred_element_type=jnp.float32
    )
    return (row_max, row_sum, weighted)


def merge_state(left_part, right_part):
    row_max = jnp.maximum(left_part[0], right_part[0])
    left_scale = jnp.exp(left_part[0] - row_max)
    right_scale = jnp.exp(right_part[0] - row_max)
    row_sum = left_part[1] * left_scale + right_part[1] * right_scale
    weighted = left_part[2] * left_scale[:, :, None] + right_part[2] * right_scale[:, :, None]
    return (row_max, row_sum, weighted)


def blank_state(count):
    return (
        jnp.full((count, BLOCK), NEG, jnp.float32),
        jnp.zeros((count, BLOCK), jnp.float32),
        jnp.zeros((count, BLOCK, HEAD_DIM), jnp.float32),
    )


def head_range(state, head_lo, head_hi):
    return tuple((member[head_lo:head_hi] for member in state))


def on_device(queries, key_states, value_states, key_keep, summary_pos):
    stride = lax.axis_size("seq")
    groups = lax.axis_size("grp")
    column = lax.axis_index("seq")
    window = lax.axis_index("grp")
    block_id = window * stride + column
    lane_ids = jnp.arange(BLOCK, dtype=jnp.int32)
    group_ids = jnp.arange(groups, dtype=jnp.int32)
    query_heads = queries.reshape(BLOCK, HEADS, HEAD_DIM)
    keep_flag = key_keep.astype(jnp.bfloat16)
    own_block = (key_states, value_states, keep_flag)

    def all_heads(block_rows, allowed):
        return partial_softmax(
            query_heads,
            block_rows[0].reshape(BLOCK, HEADS, HEAD_DIM),
            block_rows[1].reshape(BLOCK, HEADS, HEAD_DIM),
            allowed,
        )

    diagonal = lane_ids[:, None] == lane_ids[None, :]
    causal = (lane_ids[None, :] <= lane_ids[:, None]) & ((key_keep[None, :] == 1) | diagonal)
    near_state = all_heads(own_block, causal)
    prior_one = passed_along((own_block[0], own_block[1], own_block[2]), ("grp", "seq"), 1)
    prior_two = passed_along((own_block[0], own_block[1], own_block[2]), ("grp", "seq"), 2)
    for earlier in (prior_one, prior_two):
        allowed = jnp.broadcast_to((earlier[2] > 0)[None, :], (BLOCK, BLOCK))
        near_state = merge_state(near_state, all_heads(earlier, allowed))
    fixed_lo = LOCAL_HEADS * HEAD_DIM
    fixed_hi = (LOCAL_HEADS + FIXED_HEADS) * HEAD_DIM
    root_dev = summary_pos[window]
    summary_own = (key_states[:, fixed_lo:fixed_hi], value_states[:, fixed_lo:fixed_hi], keep_flag)
    summary_here = (
        spread(summary_own[0], "seq", root_dev),
        spread(summary_own[1], "seq", root_dev),
        spread(summary_own[2], "seq", root_dev),
    )
    fixed_queries = query_heads[:, LOCAL_HEADS : LOCAL_HEADS + FIXED_HEADS]
    shard_rows = (
        lax.all_gather(summary_here[0], "grp", axis=0, tiled=True),
        lax.all_gather(summary_here[1], "grp", axis=0, tiled=True),
        lax.all_gather(summary_here[2], "grp", axis=0, tiled=True),
    )
    row_count = shard_rows[0].shape[0]
    row_window = jnp.arange(row_count, dtype=jnp.int32) // BLOCK
    hit_mask = row_window[:, None] == group_ids[None, :]
    row_summary = jnp.sum(jnp.where(hit_mask, summary_pos[None, :], 0), axis=1)
    usable = (row_window * stride + row_summary < block_id - LOOKBACK) & (shard_rows[2] > 0)
    allowed = jnp.broadcast_to(usable[None, :], (BLOCK, row_count))
    term = partial_softmax(
        fixed_queries,
        shard_rows[0].reshape(row_count, FIXED_HEADS, HEAD_DIM),
        shard_rows[1].reshape(row_count, FIXED_HEADS, HEAD_DIM),
        allowed,
    )
    fixed_state = merge_state(blank_state(FIXED_HEADS), term)
    column_own = (key_states[:, fixed_hi:], value_states[:, fixed_hi:], keep_flag)
    strided_queries = query_heads[:, LOCAL_HEADS + FIXED_HEADS :]
    shard_rows = (
        lax.all_gather(column_own[0], "grp", axis=0, tiled=True),
        lax.all_gather(column_own[1], "grp", axis=0, tiled=True),
        lax.all_gather(column_own[2], "grp", axis=0, tiled=True),
    )
    row_count = shard_rows[0].shape[0]
    row_window = jnp.arange(row_count, dtype=jnp.int32) // BLOCK
    usable = (row_window < window) & (shard_rows[2] > 0)
    allowed = jnp.broadcast_to(usable[None, :], (BLOCK, row_count))
    term = partial_softmax(
        strided_queries,
        shard_rows[0].reshape(row_count, STRIDED_HEADS, HEAD_DIM),
        shard_rows[1].reshape(row_count, STRIDED_HEADS, HEAD_DIM),
        allowed,
    )
    strided_state = merge_state(blank_state(STRIDED_HEADS), term)
    local_total = head_range(near_state, 0, LOCAL_HEADS)
    fixed_total = merge_state(
        head_range(near_state, LOCAL_HEADS, LOCAL_HEADS + FIXED_HEADS), fixed_state
    )
    strided_total = merge_state(
        head_range(near_state, LOCAL_HEADS + FIXED_HEADS, HEADS), strided_state
    )
    row_sum = jnp.concatenate([local_total[1], fixed_total[1], strided_total[1]], axis=0)
    weighted = jnp.concatenate([local_total[2], fixed_total[2], strided_total[2]], axis=0)
    result = weighted / row_sum[:, :, None]
    return jnp.transpose(result, (1, 0, 2)).reshape(BLOCK, HEADS * HEAD_DIM).astype(jnp.bfloat16)


def solution(mesh):
    return jax.shard_map(
        on_device,
        mesh=mesh,
        in_specs=(
            P(("grp", "seq"), None),
            P(("grp", "seq"), None),
            P(("grp", "seq"), None),
            P(("grp", "seq")),
            P(),
        ),
        out_specs=P(("grp", "seq"), None),
        check_vma=False,
    )
```

profile of v0, /device:TPU:1, one launch (start us, length us, event | category | flops | bytes accessed | tf_op | source)
XLA Modules:
  0.0 1218.3 jit_solution(5872520702400437514)
XLA Ops:
  7.4 2.3 copy.80
  9.7 1.6 copy.117
  11.3 0.7 dynamic_slice.3
  12.6 1.8 slice_select_fusion.1
  14.4 0.7 slice_select_fusion
  15.2 1.6 slice.52
  16.8 0.5 all-gather.11.cloned.1.call-update
  17.4 559.2 %all-reduce.3.cloned.1.call-done = (bf16[128,512]{0,1:T(8,128)(2,1)}, bf16[128,512]{0,1:T(8,128)(2,1)}) async-done(((bf16[128,512]{0,1:T(8,128)(2,1)}, bf16[128,512]{0,1:T(8,128)(2,1)}), (bf16[128,512]{0,1:T(8,128)(2,1)}, bf16[128,512]{0,1:T(8,128)(2,1)})) %all-reduce.3.cloned.1.call-update) | async-done | bytes 262160 | tf_op jit(solution)/shard_map/psum | solution.py:25
  576.7 2.1 collective-permute-start.2
  578.8 1.9 collective-permute-start.1
  580.7 1.9 collective-permute-start.5
  582.6 1.9 collective-permute-start.4
  584.6 1.9 collective-permute-start
  586.5 0.4 copy.75
  586.9 282.3 %psum.21 = bf16[128]{0:T(256)(128)(2,1)S(1)} all-reduce(bf16[128]{0:T(256)(128)(2,1)S(1)} %broadcast_select_fusion), channel_id=1, replica_groups=mesh['grp'=16,'seq'=32] {'seq'}, use_global_device_ids=true, to_apply=%region_4.5 | all-reduce | flops 128 | bytes 512 | tf_op jit(solution)/shard_map/psum | solution.py:25
  869.2 219.4 %all-gather = bf16[16,1,128]{2,1,0:T(2,128)(2,1)S(1)} all-gather(bf16[1,1,128]{2,1,0:T(2,128)(2,1)S(1)} %bitcast.74), channel_id=1, replica_groups=mesh['grp'=16,'seq'=32] {'grp'}, dimensions={0}, use_global_device_ids=true | all-gather | bytes 4352 | tf_op jit(solution)/shard_map/all_gather | solution.py:104
  1088.7 25.1 %all-gather.1 = bf16[16,1,128]{2,1,0:T(2,128)(2,1)S(1)} all-gather(bf16[1,1,128]{2,1,0:T(2,128)(2,1)S(1)} %get-tuple-element.36), channel_id=1, replica_groups=mesh['grp'=16,'seq'=32] {'grp'}, dimensions={0}, use_global_device_ids=true | all-gather | bytes 4352 | tf_op jit(solution)/shard_map/all_gather | solution.py:124
  1113.8 0.1 select_reduce_fusion
  1113.9 0.1 fusion.63
  1114.0 0.4 fusion.95
  1114.4 0.4 fusion.42
  1114.8 0.3 fusion.15
  1115.1 2.1 collective-permute-start.3
  1117.3 16.0 %collective-permute-done.3 = bf16[128]{0:T(256)(128)(2,1)S(1)} collective-permute-done((bf16[128]{0:T(256)(128)(2,1)S(1)}, bf16[128]{0:T(256)(128)(2,1)S(1)}, u32[]{:S(2)}, u32[]{:S(2)}) %collective-permute-start.3) | collective-permute-done | bytes 288 | tf_op jit(solution)/shard_map/ppermute | solution.py:20
  1133.3 1.5 copy.83
  1134.8 2.3 copy.88
  1137.1 1.6 fusion.96
  1138.7 0.3 fusion.19
  1139.0 1.6 fusion.94
  1140.6 0.3 fusion.17
  1141.0 0.5 fusion.40
  1141.4 0.7 copy-done.5
  1142.1 0.7 multiply_add_fusion
  1142.8 1.2 copy-done.1
  1144.0 3.9 copy.101
  1147.9 2.7 fusion.2
  1150.7 2.0 copy-done.3
  1152.6 1.2 fusion.3
  1153.8 2.9 bitcast_reduce_fusion
  1156.8 1.6 fusion.5
  1158.4 0.5 copy-done
  1159.0 0.4 copy-done.2
  1159.4 1.0 copy-done.6
  1160.4 1.7 fusion.55
  1162.1 43.3 %all-gather.9.cloned.1.call-done = bf16[2048,512]{0,1:T(8,128)(2,1)} async-done(((bf16[128,512]{0,1:T(8,128)(2,1)}), bf16[2048,512]{0,1:T(8,128)(2,1)}) %all-gather.9.cloned.1.call-update) | async-done | bytes 2097168 | tf_op jit(solution)/shard_map/all_gather | solution.py:103
  1205.4 4.0 fusion.56
  1209.4 0.2 fusion.14
  1209.6 1.2 copy.103
  (47 shorter events, 0.4 us)
Async XLA Ops:
  7.4 569.2 %all-reduce.3.cloned.1.call-start = ((), (), s32[]{:S(2)}) async-start(), calls=%async_computation.4 | async-start | bytes 524288 | tf_op jit(solution)/shard_map/psum | solution.py:25
  7.4 3.9 copy-start.9
  9.7 574.9 %copy-start.10 = (s32[128]{0:T(128)S(1)}, s32[128]{0:T(128)}, u32[]{:S(2)}) copy-start(s32[128]{0:T(128)} %param.8) | copy-start | bytes 1540
  9.7 576.9 %copy-start.7 = (bf16[128,3072]{1,0:T(8,128)(2,1)S(1)}, bf16[128,3072]{1,0:T(8,128)(2,1)}, u32[]{:S(2)}) copy-start(bf16[128,3072]{1,0:T(8,128)(2,1)} %param.5) | copy-start | bytes 2359300
  12.6 1101.4 %copy-start.8 = (bf16[128,3072]{1,0:T(8,128)(2,1)S(1)}, bf16[128,3072]{1,0:T(8,128)(2,1)}, u32[]{:S(2)}) copy-start(bf16[128,3072]{1,0:T(8,128)(2,1)} %param.6) | copy-start | bytes 2359300
  15.1 1128.9 %all-gather.13.cloned.1.call-start = ((), (), s32[]{:S(2)}) async-start(), calls=%async_computation.3 | async-start | bytes 2228224 | tf_op jit(solution)/shard_map/all_gather | solution.py:123
  16.7 1131.2 %all-gather.11.cloned.1.call-start = ((), (), s32[]{:S(2)}) async-start(), calls=%async_computation.2 | async-start | bytes 2228224 | tf_op jit(solution)/shard_map/all_gather | solution.py:122
  17.3 1136.5 %all-gather.7.cloned.1.call-start = ((), (), s32[]{:S(2)}) async-start(), calls=%async_computation | async-start | bytes 2228224 | tf_op jit(solution)/shard_map/all_gather | solution.py:102
  576.6 628.8 %all-gather.9.cloned.1.call-start = ((), (), s32[]{:S(2)}) async-start(), calls=%async_computation.1 | async-start | bytes 2228224 | tf_op jit(solution)/shard_map/all_gather | solution.py:103
  576.7 556.6 %collective-permute-start.2 = (bf16[128,3072]{1,0:T(8,128)(2,1)}, bf16[128,3072]{1,0:T(8,128)(2,1)}, u32[]{:S(2)}, u32[]{:S(2)}) collective-permute-start(bf16[128,3072]{1,0:T(8,128)(2,1)} %param.7), channel_id=1, source_target_pairs={{0,1},{1,2},{2,3},{3,4},{4,5},{5,6},{6,7},{7,8},{8,9},{9,10},{10,1... | collective-permute-start | bytes 2359304 | tf_op jit(solution)/shard_map/ppermute | solution.py:20
  578.8 560.2 %collective-permute-start.1 = (bf16[128,3072]{0,1:T(8,128)(2,1)}, bf16[128,3072]{0,1:T(8,128)(2,1)}, u32[]{:S(2)}, u32[]{:S(2)}) collective-permute-start(bf16[128,3072]{0,1:T(8,128)(2,1)} %copy.80), channel_id=1, source_target_pairs={{0,1},{1,2},{2,3},{3,4},{4,5},{5,6},{6,7},{7,8},{8,9},{9,10},{10,1... | collective-permute-start | bytes 2359304 | tf_op jit(solution)/shard_map/ppermute | solution.py:20
  580.7 554.1 %collective-permute-start.5 = (bf16[128,3072]{1,0:T(8,128)(2,1)}, bf16[128,3072]{1,0:T(8,128)(2,1)}, u32[]{:S(2)}, u32[]{:S(2)}) collective-permute-start(bf16[128,3072]{1,0:T(8,128)(2,1)} %param.7), channel_id=1, source_target_pairs={{0,2},{1,3},{2,4},{3,5},{4,6},{5,7},{6,8},{7,9},{8,10},{9,11},{10,... | collective-permute-start | bytes 2359304 | tf_op jit(solution)/shard_map/ppermute | solution.py:20
  582.6 554.4 %collective-permute-start.4 = (bf16[128,3072]{0,1:T(8,128)(2,1)}, bf16[128,3072]{0,1:T(8,128)(2,1)}, u32[]{:S(2)}, u32[]{:S(2)}) collective-permute-start(bf16[128,3072]{0,1:T(8,128)(2,1)} %copy.80), channel_id=1, source_target_pairs={{0,2},{1,3},{2,4},{3,5},{4,6},{5,7},{6,8},{7,9},{8,10},{9,11},{10,... | collective-permute-start | bytes 2359304 | tf_op jit(solution)/shard_map/ppermute | solution.py:20
  584.6 530.5 %collective-permute-start = (bf16[128]{0:T(256)(128)(2,1)S(1)}, bf16[128]{0:T(256)(128)(2,1)S(1)}, u32[]{:S(2)}, u32[]{:S(2)}) collective-permute-start(bf16[128]{0:T(256)(128)(2,1)S(1)} %get-tuple-element.37), channel_id=1, source_target_pairs={{0,1},{1,2},{2,3},{3,4},{4,5},{5,6},{6,7},{7,8},{8,9},{9,10},{10,1... | collective-permute-start | bytes 776 | tf_op jit(solution)/shard_map/ppermute | solution.py:20
  1115.1 18.1 %collective-permute-start.3 = (bf16[128]{0:T(256)(128)(2,1)S(1)}, bf16[128]{0:T(256)(128)(2,1)S(1)}, u32[]{:S(2)}, u32[]{:S(2)}) collective-permute-start(bf16[128]{0:T(256)(128)(2,1)S(1)} %get-tuple-element.37), channel_id=1, source_target_pairs={{0,2},{1,3},{2,4},{3,5},{4,6},{5,7},{6,8},{7,9},{8,10},{9,11},{10,... | collective-permute-start | bytes 776 | tf_op jit(solution)/shard_map/ppermute | solution.py:20
  1141.0 1.1 copy-start.5
  1142.8 1.2 copy-start.1
  1150.6 2.0 copy-start.3
  1153.8 5.1 copy-start.4
  1156.8 2.1 copy-start
  1156.8 2.6 copy-start.2
  1156.8 3.6 copy-start.6
  1205.4 4.0 slice-start
Sparse Core Ops, SparseCore 0:
  15.2 561.3 all-reduce.2
Sparse Core Ops, SparseCore 1:
  17.7 107.5 all-gather.12
  127.1 84.2 all-gather.10
  576.7 299.0 all-gather.6
  1133.3 72.0 all-gather.8
where the time goes:
time: 1220 us
  waiting for transfers between devices  619 us (51%)
  blocking collectives  527 us (43%)
  local copies, waits for them, and re-layouts  21.1 us (2%)
  matrix products  16.4 us (1%)
  between operations  16.2 us (1%)
    psum x1, waiting for transfers between devices, spread(): return lax.psum(kept, axis)  559 us
    psum x1, blocking collectives, spread(): return lax.psum(kept, axis)  282 us
    all_gather x1, blocking collectives, on_device(): lax.all_gather(summary_here[2], 'grp', axis=0, tiled=True)  219 us
    all_gather x1, waiting for transfers between devices, on_device(): lax.all_gather(summary_here[1], 'grp', axis=0, tiled=True)  43.3 us
    all_gather x1, blocking collectives, on_device(): lax.all_gather(column_own[2], 'grp', axis=0, tiled=True)  25.1 us
  transfers between devices with their start and end apart: 11, of which 3 were waited for; matrix products, arithmetic and copies ran while one was open for 2% of the time, Pallas kernels for 0%

commit v1 on v0

--- a/solution.py
+++ b/solution.py
@@ -22,7 +22,7 @@
 
 def spread(value, axis, source):
     kept = jnp.where(lax.axis_index(axis) == source, value, 0).astype(value.dtype)
-    return lax.psum(kept, axis)
+    return jnp.sum(lax.all_gather(kept, axis), axis=0)
 
 
 def partial_softmax(query_heads, key_rows, value_rows, allowed):

time: 1220 us -> 1060 us (0.87)
  waiting for transfers between devices: 619 us -> 457 us
    psum x1 -> x0, waiting for transfers between devices: 559 us -> none  [spread(): return lax.psum(kept, axis)]
    all_gather x0 -> x1, blocking collectives: none -> 351 us  [spread(): return jnp.sum(lax.all_gather(kept, axis), axis=0)]
    psum x1 -> x0, blocking collectives: 282 us -> none  [spread(): return lax.psum(kept, axis)]
    all_gather x0 -> x2, waiting for transfers between devices: none -> 162 us  [spread(): return jnp.sum(lax.all_gather(kept, axis), axis=0)]
    all_gather x1, waiting for transfers between devices: 0.03 us -> 96.4 us  [on_device(): lax.all_gather(summary_here[0], 'grp', axis=0, tiled=True)]
    all_gather x1, waiting for transfers between devices: 0.01 us -> 82.3 us  [on_device(): lax.all_gather(column_own[0], 'grp', axis=0, tiled=True)]
    all_gather x1, blocking collectives: 219 us -> 139 us  [on_device(): lax.all_gather(summary_here[2], 'grp', axis=0, tiled=True)]
    all_gather x1, waiting for transfers between devices: 43.3 us -> 93.4 us  [on_device(): lax.all_gather(summary_here[1], 'grp', axis=0, tiled=True)]
  transfers between devices with their start and end apart: 11 -> 12, of which waited for: 3 -> 6; matrix products, arithmetic and copies ran while one was open for 2% -> 4% of each run, Pallas kernels for 0% -> 0%
where the time goes in v1:
time: 1060 us
  blocking collectives  515 us (49%)
  waiting for transfers between devices  457 us (43%)
  local copies, waits for them, and re-layouts  29.7 us (3%)
  matrix products  17.3 us (2%)
  other arithmetic  14.5 us (1%)
  between operations  14.5 us (1%)
  starting transfers between devices  14.4 us (1%)
    all_gather x1, blocking collectives, spread(): return jnp.sum(lax.all_gather(kept, axis), axis=0)  351 us
    all_gather x2, waiting for transfers between devices, spread(): return jnp.sum(lax.all_gather(kept, axis), axis=0)  162 us
    all_gather x1, blocking collectives, on_device(): lax.all_gather(summary_here[2], 'grp', axis=0, tiled=True)  139 us
    all_gather x1, waiting for transfers between devices, on_device(): lax.all_gather(summary_here[0], 'grp', axis=0, tiled=True)  96.4 us
    all_gather x1, waiting for transfers between devices, on_device(): lax.all_gather(summary_here[1], 'grp', axis=0, tiled=True)  93.4 us
    all_gather x1, waiting for transfers between devices, on_device(): lax.all_gather(column_own[0], 'grp', axis=0, tiled=True)  82.3 us
    all_gather x1, blocking collectives, on_device(): lax.all_gather(column_own[2], 'grp', axis=0, tiled=True)  25.1 us
  transfers between devices with their start and end apart: 12, of which 6 were waited for; matrix products, arithmetic and copies ran while one was open for 4% of the time, Pallas kernels for 0%

profile of v1, /device:TPU:1, one launch (start us, length us, event | category | flops | bytes accessed | tf_op | source)
XLA Modules:
  0.0 1062.3 jit_solution(15254386819138062917)
XLA Ops:
  6.5 1.3 dynamic_slice.3
  8.5 1.6 slice_select_fusion.1
  10.2 1.7 slice_select_fusion
  11.9 0.7 all-gather.19.cloned.1.call-update
  12.7 1.2 copy.77
  13.9 1.6 slice.62
  15.5 162.0 %all-gather.21.cloned.1.call-done = bf16[4096,512]{1,0:T(8,128)(2,1)} async-done(((bf16[128,512]{1,0:T(8,128)(2,1)}), bf16[4096,512]{1,0:T(8,128)(2,1)}) %all-gather.21.cloned.1.call-update) | async-done | bytes 4194320 | tf_op jit(solution)/shard_map/all_gather | solution.py:25
  177.5 3.5 reduce_sum.92
  181.1 1.9 collective-permute-start.2
  183.0 4.1 collective-permute-start.1
  187.1 2.3 collective-permute-start.5
  189.4 1.9 collective-permute-start.4
  191.3 1.9 collective-permute-start
  193.6 1.5 copy.72
  195.2 351.1 %all-gather.3 = bf16[32,1,128]{2,1,0:T(2,128)(2,1)S(1)} all-gather(bf16[1,1,128]{2,1,0:T(2,128)(2,1)S(1)} %fusion.81), channel_id=2, replica_groups=mesh['grp'=16,'seq'=32] {'seq'}, dimensions={0}, use_global_device_ids=true | all-gather | bytes 8448 | tf_op jit(solution)/shard_map/all_gather | solution.py:25
  546.3 138.8 %all-gather.4 = bf16[16,1,128]{2,1,0:T(2,128)(2,1)S(1)} all-gather(bf16[1,1,128]{2,1,0:T(2,128)(2,1)S(1)} %bitcast.81), channel_id=1, replica_groups=mesh['grp'=16,'seq'=32] {'grp'}, dimensions={0}, use_global_device_ids=true | all-gather | bytes 4352 | tf_op jit(solution)/shard_map/all_gather | solution.py:104
  685.1 25.1 %all-gather.5 = bf16[16,1,128]{2,1,0:T(2,128)(2,1)S(1)} all-gather(bf16[1,1,128]{2,1,0:T(2,128)(2,1)S(1)} %get-tuple-element.34), channel_id=1, replica_groups=mesh['grp'=16,'seq'=32] {'grp'}, dimensions={0}, use_global_device_ids=true | all-gather | bytes 4352 | tf_op jit(solution)/shard_map/all_gather | solution.py:124
  710.4 1.5 fusion.96
  711.9 1.6 fusion.42
  713.8 2.1 collective-permute-start.3
  716.0 16.0 %collective-permute-done.3 = bf16[128]{0:T(256)(128)(2,1)S(1)} collective-permute-done((bf16[128]{0:T(256)(128)(2,1)S(1)}, bf16[128]{0:T(256)(128)(2,1)S(1)}, u32[]{:S(2)}, u32[]{:S(2)}) %collective-permute-start.3) | collective-permute-done | bytes 288 | tf_op jit(solution)/shard_map/ppermute | solution.py:20
  731.9 2.3 copy.80
  734.2 2.3 copy.85
  736.5 1.6 fusion.97
  738.5 3.5 reduce_sum.93
  742.0 1.6 fusion.95
  744.0 0.8 copy-done.6
  745.2 1.0 copy-done.1
  746.4 0.7 multiply_add_fusion
  747.1 1.2 copy-done.2
  748.3 6.2 all-gather.19.cloned.1.call-done
  754.5 3.9 copy.98
  758.4 82.3 %all-gather.17.cloned.1.call-done = bf16[2048,512]{0,1:T(8,128)(2,1)} async-done(((bf16[128,512]{0,1:T(8,128)(2,1)}), bf16[2048,512]{0,1:T(8,128)(2,1)}) %all-gather.17.cloned.1.call-update) | async-done | bytes 2097168 | tf_op jit(solution)/shard_map/all_gather | solution.py:122
  840.7 2.7 fusion.2
  843.4 1.9 copy-done.4
  845.3 1.2 fusion.3
  846.5 96.4 %all-gather.13.cloned.1.call-done = bf16[2048,512]{1,0:T(8,128)(2,1)} async-done(((bf16[128,512]{1,0:T(8,128)(2,1)}), bf16[2048,512]{1,0:T(8,128)(2,1)}) %all-gather.13.cloned.1.call-update) | async-done | bytes 2097168 | tf_op jit(solution)/shard_map/all_gather | solution.py:102
  942.9 2.9 copy.88
  945.8 1.5 bitcast_reduce_fusion
  947.3 1.6 fusion.5
  948.9 0.5 copy-done
  949.5 0.5 copy-done.3
  950.0 1.0 copy-done.8
  951.0 1.7 fusion.55
  952.8 93.4 %all-gather.15.cloned.1.call-done = bf16[2048,512]{1,0:T(8,128)(2,1)} async-done(((bf16[128,512]{1,0:T(8,128)(2,1)}), bf16[2048,512]{1,0:T(8,128)(2,1)}) %all-gather.15.cloned.1.call-update) | async-done | bytes 2097168 | tf_op jit(solution)/shard_map/all_gather | solution.py:103
  1046.1 4.0 copy.91
  1050.2 4.0 fusion.56
  1054.3 1.2 copy.100
  (59 shorter events, 2.8 us)
Async XLA Ops:
  6.5 6.1 copy-start.10
  6.5 170.9 %all-gather.21.cloned.1.call-start = ((), (), s32[]{:S(2)}) async-start(), calls=%async_computation.4 | async-start | bytes 4325376 | tf_op jit(solution)/shard_map/all_gather | solution.py:25
  10.1 728.4 %all-gather.23.cloned.1.call-start = ((), (), s32[]{:S(2)}) async-start(), calls=%async_computation.5 | async-start | bytes 4325376 | tf_op jit(solution)/shard_map/all_gather | solution.py:25
  11.9 742.6 %all-gather.19.cloned.1.call-start = ((), (), s32[]{:S(2)}) async-start(), calls=%async_computation.3 | async-start | bytes 2228224 | tf_op jit(solution)/shard_map/all_gather | solution.py:123
  12.6 828.1 %all-gather.17.cloned.1.call-start = ((), (), s32[]{:S(2)}) async-start(), calls=%async_computation.2 | async-start | bytes 2228224 | tf_op jit(solution)/shard_map/all_gather | solution.py:122
  15.4 927.4 %all-gather.13.cloned.1.call-start = ((), (), s32[]{:S(2)}) async-start(), calls=%async_computation | async-start | bytes 2228224 | tf_op jit(solution)/shard_map/all_gather | solution.py:102
  177.5 3.6 copy-start.9
  177.5 13.8 %copy-start.12 = (s32[128]{0:T(128)S(1)}, s32[128]{0:T(128)}, u32[]{:S(2)}) copy-start(s32[128]{0:T(128)} %param.8) | copy-start | bytes 1540
  181.0 865.1 %all-gather.15.cloned.1.call-start = ((), (), s32[]{:S(2)}) async-start(), calls=%async_computation.1 | async-start | bytes 2228224 | tf_op jit(solution)/shard_map/all_gather | solution.py:103
  181.1 550.8 %collective-permute-start.2 = (bf16[128,3072]{1,0:T(8,128)(2,1)S(1)}, bf16[128,3072]{1,0:T(8,128)(2,1)}, u32[]{:S(2)}, u32[]{:S(2)}) collective-permute-start(bf16[128,3072]{1,0:T(8,128)(2,1)S(1)} %copy-done.9), channel_id=1, source_target_pairs={{0,1},{1,2},{2,3},{3,4},{4,5},{5,6},{6,7},{7,8},{8,9},{9,10},{10,1... | collective-permute-start | bytes 2359304 | tf_op jit(solution)/shard_map/ppermute | solution.py:20
  183.0 559.0 %collective-permute-start.1 = (bf16[128,3072]{0,1:T(8,128)(2,1)}, bf16[128,3072]{0,1:T(8,128)(2,1)}, u32[]{:S(2)}, u32[]{:S(2)}) collective-permute-start(bf16[128,3072]{0,1:T(8,128)(2,1)} %copy.77), channel_id=1, source_target_pairs={{0,1},{1,2},{2,3},{3,4},{4,5},{5,6},{6,7},{7,8},{8,9},{9,10},{10,1... | collective-permute-start | bytes 2359304 | tf_op jit(solution)/shard_map/ppermute | solution.py:20
  187.1 547.1 %collective-permute-start.5 = (bf16[128,3072]{1,0:T(8,128)(2,1)S(1)}, bf16[128,3072]{1,0:T(8,128)(2,1)}, u32[]{:S(2)}, u32[]{:S(2)}) collective-permute-start(bf16[128,3072]{1,0:T(8,128)(2,1)S(1)} %copy-done.9), channel_id=1, source_target_pairs={{0,2},{1,3},{2,4},{3,5},{4,6},{5,7},{6,8},{7,9},{8,10},{9,11},{10,... | collective-permute-start | bytes 2359304 | tf_op jit(solution)/shard_map/ppermute | solution.py:20
  189.4 547.2 %collective-permute-start.4 = (bf16[128,3072]{0,1:T(8,128)(2,1)}, bf16[128,3072]{0,1:T(8,128)(2,1)}, u32[]{:S(2)}, u32[]{:S(2)}) collective-permute-start(bf16[128,3072]{0,1:T(8,128)(2,1)} %copy.77), channel_id=1, source_target_pairs={{0,2},{1,3},{2,4},{3,5},{4,6},{5,7},{6,8},{7,9},{8,10},{9,11},{10,... | collective-permute-start | bytes 2359304 | tf_op jit(solution)/shard_map/ppermute | solution.py:20
  191.3 518.9 %copy-start.11 = (s32[16]{0:T(128)S(1)}, s32[16]{0:T(128)}, u32[]{:S(2)}) copy-start(s32[16]{0:T(128)} %param.9) | copy-start | bytes 196
  191.3 522.5 %collective-permute-start = (bf16[128]{0:T(256)(128)(2,1)S(1)}, bf16[128]{0:T(256)(128)(2,1)S(1)}, u32[]{:S(2)}, u32[]{:S(2)}) collective-permute-start(bf16[128]{0:T(256)(128)(2,1)S(1)} %get-tuple-element.35), channel_id=1, source_target_pairs={{0,1},{1,2},{2,3},{3,4},{4,5},{5,6},{6,7},{7,8},{8,9},{9,10},{10,1... | collective-permute-start | bytes 776 | tf_op jit(solution)/shard_map/ppermute | solution.py:20
  713.8 18.1 %collective-permute-start.3 = (bf16[128]{0:T(256)(128)(2,1)S(1)}, bf16[128]{0:T(256)(128)(2,1)S(1)}, u32[]{:S(2)}, u32[]{:S(2)}) collective-permute-start(bf16[128]{0:T(256)(128)(2,1)S(1)} %get-tuple-element.35), channel_id=1, source_target_pairs={{0,2},{1,3},{2,4},{3,5},{4,6},{5,7},{6,8},{7,9},{8,10},{9,11},{10,... | collective-permute-start | bytes 776 | tf_op jit(solution)/shard_map/ppermute | solution.py:20
  743.6 1.1 copy-start.6
  744.7 1.4 copy-start.1
  744.7 1.6 copy-start.7
  747.1 1.2 copy-start.2
  843.4 2.0 copy-start.4
  945.8 3.7 copy-start.5
  947.3 2.1 copy-start
  947.3 2.7 copy-start.3
  947.3 3.7 copy-start.8
  1050.1 4.0 slice-start
Sparse Core Ops, SparseCore 0:
  11.8 165.6 all-gather.20
  181.9 472.0 all-gather.22
  656.1 98.3 all-gather.18
  756.3 84.3 all-gather.16
  842.6 100.2 all-gather.12
  944.8 101.3 all-gather.14
